TPU v7x, 256 devices: a whole 4x4x8 slice. The times are simulated.
256 devices in a mesh: space: 64 (over z, y, core), tm: 4 (over x).
Axes of the slice: x: 4, y: 4, z: 8, core: 2. Of those that a mesh axis runs over, the one named last changes fastest.
Arguments:
- snapshots: bfloat16 [256, 524288], P('tm', 'space'), may hold values from -75 to 75
- prior_basis: bfloat16 [256, 524288], P('tm', 'space'), may hold values from -75 to 75
- mass_factor: bfloat16 [7, 64, 524288], P(None, None, 'space'), may hold values from -1 to 3.2, as said below
- neighbours: int32 [8192, 7], P('space'), may hold values from 0 to 8191, as said below
Outputs:
- merged_basis: bfloat16 [64, 524288], P(None, ('space', 'tm'))
- merged_weighted: bfloat16 [64, 524288], P(None, ('space', 'tm'))
Inputs may be any that keep to these rules, and one draw needn't show every extreme that they name: `mass_factor`: factor entries; the diagonal of each block's own coupling lies in 1.5 to 3. neighbours[i, 0] = i; every entry lies within 8 blocks of i; in every draw some entries lie exactly 8 blocks below and above their block.
All inputs are finite; a program needn't handle non-finite values.
Results may differ from a plain program's by a relative error of at most 0.018.
Values may be sent and summed in bfloat16 or wider, within the bound.
A program may use at most 128 MiB of HBM per device.

v0:
```python
import functools

import jax
import jax.numpy as jnp
from jax import lax
from jax.experimental import pallas as pl
from jax.experimental.pallas import tpu as pltpu
from jax.sharding import PartitionSpec as P

BLOCK = 64
RANK = 64
NEIGHBOURS = 7
REACH = 8
STEPS = 3
LOCAL_BLOCKS = 128
N_SPACE = 64
N_TM = 4
ROWS = 128
SLAB = LOCAL_BLOCKS * BLOCK
SHARE = SLAB // N_TM
HALO = REACH * BLOCK
WINDOW = SHARE + 2 * HALO
SHARE_BLOCKS = SHARE // BLOCK
TILES = WINDOW // 128
WIDE = SLAB + 2 * HALO
WIDE_TILES = WIDE // 128
HALO_TILES = HALO // 128
MESH = pl.DeviceIdType.MESH
HIGHEST = lax.Precision.HIGHEST
F32 = jnp.float32
BF16 = jnp.bfloat16


def dot_nn(a, b):
    return lax.dot_general(
        a, b, (((1,), (0,)), ((), ())), precision=HIGHEST, preferred_element_type=F32
    )


def dot_nt(a, b):
    return lax.dot_general(
        a, b, (((1,), (1,)), ((), ())), precision=HIGHEST, preferred_element_type=F32
    )


def eliminate(inners):
    sub = lax.broadcasted_iota(jnp.int32, (8, 128), 0)
    lane = lax.broadcasted_iota(jnp.int32, (8, 128), 1)
    grids = []
    for inner in inners:
        tiles = []
        for i in range(8):
            unit = jnp.where(lane == 8 * i + sub + BLOCK, 1.0, 0.0).astype(F32)
            left = jnp.concatenate([inner[8 * i : 8 * i + 8, :], jnp.zeros((8, BLOCK), F32)], axis=1)
            tiles.append(left + unit)
        grids.append(tiles)
    outs = [[] for _ in inners]
    for p in range(8):
        panels = [
            [[jnp.broadcast_to(tiles[i][:, 8 * p + q : 8 * p + q + 1], (8, 128)) for q in range(8)] for i in range(p, 8)]
            for tiles in grids
        ]
        roots = [jnp.ones((8, 128), F32) for _ in grids]
        for q in range(8):
            for m, (tiles, cols) in enumerate(zip(grids, panels)):
                pivot = jnp.broadcast_to(cols[0][q][q : q + 1, :], (8, 128))
                inv = 1.0 / pivot
                roots[m] = jnp.where(sub == q, pivot, roots[m])
                for r in range(q + 1, 8):
                    factor = jnp.broadcast_to(cols[0][r][q : q + 1, :], (8, 128)) * inv
                    for i in range(8 - p):
                        cols[i][r] = cols[i][r] - cols[i][q] * factor
                row = jnp.broadcast_to(tiles[p][q : q + 1, :], (8, 128)) * inv
                for i in range(p, 8):
                    change = cols[i - p][q] * row
                    if i == p:
                        change = jnp.where(sub > q, change, 0.0)
                    tiles[i] = tiles[i] - change
        for out, tiles, root in zip(outs, grids, roots):
            out.append(tiles[p] * lax.rsqrt(root))
    return [jnp.concatenate(out, axis=0) for out in outs]


def compress(grams):
    zeros = jnp.zeros((BLOCK, ROWS), F32)

    def apply(inverse, rows):
        return dot_nn(inverse, jnp.concatenate([zeros, rows], axis=0))

    def step(_, state):
        _, _, products = state
        seconds = [dot_nn(p, g) for p, g in zip(products, grams)]
        inverses = eliminate([dot_nt(p, q) for p, q in zip(products, seconds)])
        return inverses, products, [apply(inv, q) for inv, q in zip(inverses, seconds)]

    first = [gram[:RANK, :] for gram in grams]
    state = (first, first, first)
    for i in range(STEPS):
        state = step(i, state)
    inverses, products, nexts = state
    result = []
    for inv, p, q in zip(inverses, products, nexts):
        lengths = jnp.sqrt(jnp.sum(q * q, axis=1, keepdims=True) + 1e-06)
        result.append((apply(inv, p) * lengths).astype(BF16))
    return result


def tiles_of(neighbours, s):
    at = neighbours - (s * LOCAL_BLOCKS - REACH)
    second = lax.broadcasted_iota(jnp.int32, at.shape, 0) & 1
    moved = (at & 1) ^ second
    return ((at + 1 - second) >> 1) + moved * WIDE_TILES


def pick_modes(tile, j, tiles, in_low):
    picks = []
    for k in range(NEIGHBOURS):
        low = tiles[tile[2 * j, k]]
        high = tiles[tile[2 * j + 1, k]]
        picks.append(jnp.where(in_low, low, high))
    return jnp.concatenate(picks, axis=1)


def pick_factor(j, factor, in_low):
    zero = jnp.zeros((BLOCK, 128), BF16)
    pieces = []
    for k in range(NEIGHBOURS):
        block = factor[k, :, pl.ds(pl.multiple_of(j * 128, 128), 128)]
        pieces += [jnp.where(in_low, block, zero), jnp.where(in_low, zero, block)]
    return jnp.concatenate(pieces, axis=0)


def halves(before, after):
    return jnp.concatenate([before[:, BLOCK:], after[:, :BLOCK]], axis=1)


def widen(wide, tiles, low, high, unroll):
    def one_tile(m, carry):
        before = wide[:, pl.ds(pl.multiple_of(128 * (m - 1), 128), 128)]
        after = wide[:, pl.ds(pl.multiple_of(128 * m, 128), 128)]
        tiles[m] = after
        tiles[WIDE_TILES + m] = halves(before, after)
        return carry

    lax.fori_loop(low, high, one_tile, 0, unroll=unroll)


def widen_ends(wide, tiles):
    last = wide.shape[1] // 128 - 1
    first = wide[:, pl.ds(0, 128)]
    tiles[0] = first
    tiles[WIDE_TILES] = halves(first, first)
    end = wide[:, pl.ds(128 * last, 128)]
    tiles[WIDE_TILES + last + 1] = halves(end, end)


def lowest_kernel(
    tile,
    prior,
    snaps,
    mass,
    rows_out,
    weighted_out,
    gram_out,
    own,
    own_tiles,
    weights_own,
    weights_in,
    factor,
    gram,
    r_plane,
    r_z,
    total,
    coefs,
    send_sem,
    recv_sem,
    local_sem,
    sum_send,
    sum_recv,
):
    s = lax.axis_index("space")
    t = lax.axis_index("tm")
    c = lax.rem(s, 2)
    y = lax.rem(s // 2, 4)
    z = s // 8
    up = lax.rem(s + 1, N_SPACE)
    down = lax.rem(s + N_SPACE - 1, N_SPACE)
    sources = (prior, snaps)
    chunk = SLAB // 4

    def half(part):
        return pl.ds(part * 64, 64)

    loads = [
        pltpu.make_async_copy(
            sources[part], own.at[half(part), pl.ds(HALO, SLAB)], local_sem.at[part]
        )
        for part in range(2)
    ]
    fetches = [
        pltpu.make_async_copy(
            mass.at[:, :, pl.ds(chunk * i, chunk)],
            factor.at[:, :, pl.ds(chunk * i, chunk)],
            local_sem.at[2 + i],
        )
        for i in range(4)
    ]
    for one in loads + fetches:
        one.start()

    def space_of(zz, yy, cc):
        return zz * 8 + yy * 2 + cc

    x_peers = [(s, lax.rem(t + h, 4)) for h in (1, 2, 3)]
    me = c * 4 + y
    plane = []
    for dc, dy in ((1, 2), (0, 2), (1, 1), (1, 3), (0, 1), (0, 3), (1, 0)):
        pc, py = lax.rem(c + dc, 2), lax.rem(y + dy, 4)
        plane.append((pc * 4 + py, (space_of(z, py, pc), t)))
    z_peers = [(space_of(lax.rem(z + d, 8), y, c), t) for d in range(1, 8)]

    barrier = pltpu.get_barrier_semaphore()
    for peer in x_peers + [where for _, where in plane] + z_peers + [(up, t), (down, t)]:
        pl.semaphore_signal(barrier, inc=1, device_id=peer, device_id_type=MESH)

    pl.semaphore_wait(barrier, 19)

    def remote(src, dst, slot, peer, part):
        return pltpu.make_async_remote_copy(
            src_ref=src,
            dst_ref=dst,
            send_sem=send_sem.at[slot, part],
            recv_sem=recv_sem.at[slot, part],
            device_id=peer,
            device_id_type=MESH,
        )

    def share(hop):
        return remote(
            weights_own.at[:, pl.ds(pl.multiple_of(lax.rem(t + hop, 4) * SHARE, 128), SHARE)],
            weights_in.at[hop - 1],
            hop - 1,
            x_peers[hop - 1],
            0,
        )

    def own_edge(part, side):
        low, at = (SLAB - HALO, 0) if side == 0 else (0, WIDE - HALO)
        return remote(
            sources[part].at[:, pl.ds(low, HALO)],
            own.at[half(part), pl.ds(at, HALO)],
            3 + side,
            (up, t) if side == 0 else (down, t),
            part,
        )

    for part in range(2):
        for side in range(2):
            own_edge(part, side).start()

    in_low = lax.broadcasted_iota(jnp.int32, (1, 128), 1) < BLOCK
    for one in loads:
        one.wait()
    widen(own, own_tiles, HALO_TILES + 1, WIDE_TILES - HALO_TILES, 9)
    for part in range(2):
        for side in range(2):
            own_edge(part, side).wait()
    widen(own, own_tiles, 1, HALO_TILES + 1, HALO_TILES)
    widen(own, own_tiles, WIDE_TILES - HALO_TILES, WIDE_TILES, HALO_TILES)
    widen_ends(own, own_tiles)
    for one in fetches:
        one.wait()

    def own_quarter(quarter):
        def own_tile(i, carry):
            j = quarter * (SHARE_BLOCKS // 2) + i
            modes = pick_modes(tile, j, own_tiles, in_low)
            result = jnp.dot(modes, pick_factor(j, factor, in_low), preferred_element_type=F32)
            weights_own[:, pl.ds(pl.multiple_of(j * 128, 128), 128)] = result.astype(BF16)
            return carry

        lax.fori_loop(0, SHARE_BLOCKS // 2, own_tile, 0, unroll=4)

    for hop in (2, 1, 3):
        own_quarter(lax.rem(t + hop, 4))
        share(hop).start()
    own_quarter(t)
    local = lax.dot_general(
        weights_own[...], weights_own[...], (((1,), (1,)), ((), ())), preferred_element_type=F32
    )
    for i in range(8):
        gram[i] = local[16 * i : 16 * i + 16, :]

    def over(src, dst, slot, peer):
        return pltpu.make_async_remote_copy(
            src_ref=src,
            dst_ref=dst,
            send_sem=sum_send.at[slot],
            recv_sem=sum_recv.at[slot],
            device_id=peer,
            device_id_type=MESH,
        )

    def run(copies):
        for one in copies:
            one.start()
        for one in copies:
            one.wait()

    run([over(gram.at[owner], r_plane.at[i], i, where) for i, (owner, where) in enumerate(plane)])
    piece = gram[me]
    for i in range(7):
        piece = piece + r_plane[i]
    r_z[z] = piece
    run([over(r_z.at[z], r_z.at[z], 6 + d, z_peers[d - 1]) for d in (4, 3, 5, 2, 6, 1, 7)])
    piece = r_z[0]
    for i in range(1, 8):
        piece = piece + r_z[i]
    total[me] = piece
    run([over(total.at[me], total.at[me], 14 + i, where) for i, (_, where) in enumerate(plane)])

    summed = jnp.concatenate([total[i] for i in range(8)], axis=0)
    coefs[t] = compress([summed])[0]
    passed = [remote(coefs.at[t], coefs.at[t], 4 + h, x_peers[h - 1], 0) for h in (2, 1, 3)]
    for one in passed:
        one.start()

    rows_out[...] = jnp.dot(
        coefs[t], own[:, pl.ds(HALO, SLAB)], preferred_element_type=F32
    ).astype(BF16)
    for hop in (1, 3, 2):
        share(hop).wait()

    def put(group, weighted):
        weighted_out[pl.ds(pl.multiple_of(group * RANK, RANK), RANK), :] = jnp.dot(
            coefs[group], weighted, preferred_element_type=F32
        ).astype(BF16)

    put(t, weights_own[:, pl.ds(pl.multiple_of(t * SHARE, 128), SHARE)])
    for one in passed:
        one.wait()
    for hop in (1, 2, 3):
        put(lax.rem(t + N_TM - hop, N_TM), weights_in[hop - 1])
    for a in range(2):
        for b in range(2):
            gram_out[2 * a + b] = lax.dot_general(
                weighted_out[pl.ds(a * ROWS, ROWS), :],
                weighted_out[pl.ds(b * ROWS, ROWS), :],
                (((1,), (1,)), ((), ())),
                preferred_element_type=F32,
            )


def lowest(tile, prior, snaps, mass):
    piece = (16, 128)
    vmem = pl.BlockSpec(memory_space=pltpu.VMEM)
    anywhere = pl.BlockSpec(memory_space=pl.ANY)
    return pl.pallas_call(
        lowest_kernel,
        out_shape=(
            jax.ShapeDtypeStruct((RANK, SLAB), BF16),
            jax.ShapeDtypeStruct((N_TM * RANK, SHARE), BF16),
            jax.ShapeDtypeStruct((4, ROWS, ROWS), F32),
        ),
        in_specs=[pl.BlockSpec(memory_space=pltpu.SMEM), anywhere, anywhere, anywhere],
        out_specs=(vmem, vmem, vmem),
        scratch_shapes=[
            pltpu.VMEM((ROWS, WIDE), BF16),
            pltpu.VMEM((2 * WIDE_TILES + 1, ROWS, 128), BF16),
            pltpu.VMEM((ROWS, SLAB), BF16),
            pltpu.VMEM((3, ROWS, SHARE), BF16),
            pltpu.VMEM((NEIGHBOURS, BLOCK, SLAB), BF16),
            pltpu.VMEM((8,) + piece, F32),
            pltpu.VMEM((7,) + piece, F32),
            pltpu.VMEM((8,) + piece, F32),
            pltpu.VMEM((8,) + piece, F32),
            pltpu.VMEM((N_TM, RANK, ROWS), BF16),
            pltpu.SemaphoreType.DMA((8, 2)),
            pltpu.SemaphoreType.DMA((8, 2)),
            pltpu.SemaphoreType.DMA((6,)),
            pltpu.SemaphoreType.DMA((21,)),
            pltpu.SemaphoreType.DMA((21,)),
        ],
        compiler_params=pltpu.CompilerParams(collective_id=0, has_side_effects=True),
        name="lowest",
    )(tile, prior, snaps, mass)


PIECE = 16


def reduce_kernel(
    inp,
    rows,
    out,
    rows_out,
    r_plane,
    r_z,
    plane_send,
    plane_recv,
    z_send,
    z_recv,
    rows_send,
    rows_recv,
):
    s = lax.axis_index("space")
    x = lax.axis_index("tm")
    c = lax.rem(s, 2)
    y = lax.rem(s // 2, 4)
    z = s // 8
    me = c * 16 + x * 4 + y
    hops = [(dc, dx, dy) for dx in (2, 1, 3, 0) for dy in (2, 1, 3, 0) for dc in (1, 0)]
    plane = []
    for dc, dx, dy in hops[:-1]:
        pc, px, py = lax.rem(c + dc, 2), lax.rem(x + dx, 4), lax.rem(y + dy, 4)
        plane.append((pc * 16 + px * 4 + py, (z * 8 + py * 2 + pc, px)))
    z_peers = [(lax.rem(z + d, 8) * 8 + y * 2 + c, x) for d in range(1, 8)]
    barrier = pltpu.get_barrier_semaphore()
    for peer in [where for _, where in plane] + z_peers:
        pl.semaphore_signal(barrier, inc=1, device_id=peer, device_id_type=MESH)
    pl.semaphore_wait(barrier, 38)

    def copy(src, dst, send, recv, slot, peer):
        return pltpu.make_async_remote_copy(
            src_ref=src,
            dst_ref=dst,
            send_sem=send.at[slot],
            recv_sem=recv.at[slot],
            device_id=peer,
            device_id_type=MESH,
        )

    def run(copies):
        for one in copies:
            one.start()
        for one in copies:
            one.wait()

    run(
        [
            copy(inp.at[owner], r_plane.at[i], plane_send, plane_recv, i, where)
            for i, (owner, where) in enumerate(plane)
        ]
    )
    own_rows = pl.ds(pl.multiple_of(x * RANK, RANK), RANK)

    def columns(member):
        return pl.ds(pl.multiple_of(member * SHARE, 128), SHARE)

    moved = [
        copy(
            rows.at[:, columns(lax.rem(x + hop, 4))],
            rows_out.at[own_rows, :],
            rows_send,
            rows_recv,
            hop - 1,
            (s, lax.rem(x + hop, 4)),
        )
        for hop in (2, 1, 3)
    ]
    piece = inp[me]
    for i in range(31):
        piece = piece + r_plane[i]
    r_z[z] = piece
    around = [
        copy(r_z.at[z], r_z.at[z], z_send, z_recv, d - 1, z_peers[d - 1])
        for d in (4, 3, 5, 2, 6, 1, 7)
    ]
    for one in around + moved:
        one.start()
    rows_out[own_rows, :] = rows[:, columns(x)]
    for one in around:
        one.wait()
    piece = r_z[0]
    for i in range(1, 8):
        piece = piece + r_z[i]
    out[me] = piece
    run(
        [
            copy(out.at[me], out.at[me], plane_send, plane_recv, 31 + i, where)
            for i, (_, where) in enumerate(plane)
        ]
    )
    for one in moved:
        one.wait()


def all_reduce(gram, rows):
    shape = (32, PIECE, 128)
    vmem = pl.BlockSpec(memory_space=pltpu.VMEM)
    total, gathered = pl.pallas_call(
        reduce_kernel,
        out_shape=(
            jax.ShapeDtypeStruct(shape, F32),
            jax.ShapeDtypeStruct((N_TM * RANK, SHARE), BF16),
        ),
        in_specs=[vmem, vmem],
        out_specs=(vmem, vmem),
        scratch_shapes=[
            pltpu.VMEM((31, PIECE, 128), F32),
            pltpu.VMEM((8, PIECE, 128), F32),
            pltpu.SemaphoreType.DMA((62,)),
            pltpu.SemaphoreType.DMA((62,)),
            pltpu.SemaphoreType.DMA((7,)),
            pltpu.SemaphoreType.DMA((7,)),
            pltpu.SemaphoreType.DMA((3,)),
            pltpu.SemaphoreType.DMA((3,)),
        ],
        compiler_params=pltpu.CompilerParams(collective_id=1, has_side_effects=True),
        name="all_reduce",
    )(gram.reshape(shape), rows)
    return total.reshape(4, ROWS, ROWS), gathered


def merge_kernel(gram, rows, weighted, rows_out, weighted_out, above):
    above[...] = jnp.zeros_like(above)
    second = [c.astype(F32) for c in compress([gram[0], gram[3]])]
    for p in range(2):
        above[pl.ds(p * RANK, RANK), pl.ds(p * ROWS, ROWS)] = second[p]
    mixed = [
        jnp.concatenate([dot_nn(second[p], gram[2 * p + q]) for q in range(2)], axis=1)
        for p in range(2)
    ]
    last = compress([dot_nt(jnp.concatenate(mixed, axis=0), above[...])])[0]
    mix = dot_nn(last.astype(F32), above[...]).astype(BF16)
    rows_out[...] = jnp.dot(mix, rows[...], preferred_element_type=F32).astype(BF16)
    weighted_out[...] = jnp.dot(mix, weighted[...], preferred_element_type=F32).astype(BF16)


def merge(gram, rows, weighted):
    vmem = pl.BlockSpec(memory_space=pltpu.VMEM)
    return pl.pallas_call(
        merge_kernel,
        out_shape=(jax.ShapeDtypeStruct((RANK, SHARE), BF16),) * 2,
        in_specs=[vmem] * 3,
        out_specs=(vmem, vmem),
        scratch_shapes=[pltpu.VMEM((2 * RANK, 2 * ROWS), F32)],
        name="merge",
    )(gram, rows, weighted)


def shards(snapshots, prior_basis, mass_factor, neighbours):
    tile = tiles_of(neighbours, lax.axis_index("space"))
    rows, weighted, gram = lowest(tile, prior_basis, snapshots, mass_factor)
    return merge(*all_reduce(gram, rows), weighted)


def solution(mesh):
    return jax.shard_map(
        shards,
        mesh=mesh,
        in_specs=(P("tm", "space"), P("tm", "space"), P(None, None, "space"), P("space", None)),
        out_specs=(P(None, ("space", "tm")), P(None, ("space", "tm"))),
        check_vma=False,
    )
```

profile of v0, /device:TPU:1, one launch (start us, length us, event | category | flops | bytes accessed | tf_op | source)
XLA Modules:
  0.0 101.1 jit_solution(303954421597893301)
XLA Ops:
  0.6 0.7 subtract_shift-right-arithmetic_fusion
  1.3 0.1 copy.15
  1.5 0.1 copy.13
  1.6 0.7 multiply_add_fusion.tile
  2.3 49.7 %lowest.1 = (bf16[64,8192]{1,0:T(8,128)(2,1)}, bf16[256,2048]{1,0:T(8,128)(2,1)}, f32[4,128,128]{2,1,0:T(8,128)}) custom-call(s32[128,7]{1,0:T(8,128)} %multiply_add_fusion.tile, bf16[64,8192]{1,0:T(8,128)(2,1)} %prior.1, bf16[64,8192]{1,0:T(8,128)(2,1)} %snaps.1, bf16[7,64,8192]{2,1,0:T(8,128)(2,1)} %mass.1), custom_call_target="tpu_custom_call" | custom-call | tf_op jit(solution)/shard_map/lowest/pallas_call | solution.py:358
  52.0 30.1 %all_reduce.1 = (f32[32,16,128]{2,1,0:T(8,128)}, bf16[256,2048]{1,0:T(8,128)(2,1)}) custom-call(f32[32,16,128]{2,1,0:T(8,128)} %bitcast.3, bf16[64,8192]{1,0:T(8,128)(2,1)} %get-tuple-element.8.rows), custom_call_target="tpu_custom_call" | custom-call | tf_op jit(solution)/shard_map/all_reduce/pallas_call | solution.py:491
  82.1 19.0 %merge.1 = (bf16[64,2048]{1,0:T(8,128)(2,1)}, bf16[64,2048]{1,0:T(8,128)(2,1)}) custom-call(f32[4,128,128]{2,1,0:T(8,128)} %bitcast.2, bf16[256,2048]{1,0:T(8,128)(2,1)} %get-tuple-element.10.rows, bf16[256,2048]{1,0:T(8,128)(2,1)} %get-tuple-element.11.weighted), custom_call_target="tpu_custom_call" | custom-call | tf_op jit(solution)/shard_map/merge/pallas_call | solution.py:532
  (1 shorter events, 0.0 us)
where the time goes:
time: 101 us
  Pallas kernels  98.8 us (98%)
  other arithmetic  1.42 us (1%)
    pallas_call x1, Pallas kernels, lowest(): pl.pallas_call(lowest_kernel, out_shape=(jax.ShapeDtypeStruct((RANK, SLAB...  49.7 us
    pallas_call x1, Pallas kernels, all_reduce(): pl.pallas_call(reduce_kernel, out_shape=(jax.ShapeDtypeStruct(shape, F32)...  30.1 us
    pallas_call x1, Pallas kernels, merge(): pl.pallas_call(merge_kernel, out_shape=(jax.ShapeDtypeStruct((RANK, SHARE...  19 us

commit v1 on v0

--- a/solution.py
+++ b/solution.py
@@ -389,11 +389,16 @@
 PIECE = 16
 
 
-def reduce_kernel(
+def merge_kernel(
     inp,
     rows,
+    weighted,
+    rows_out,
+    weighted_out,
     out,
-    rows_out,
+    rows_in,
+    weighted_in,
+    above,
     r_plane,
     r_z,
     plane_send,
@@ -402,6 +407,7 @@
     z_recv,
     rows_send,
     rows_recv,
+    local_sem,
 ):
     s = lax.axis_index("space")
     x = lax.axis_index("tm")
@@ -415,6 +421,17 @@
         pc, px, py = lax.rem(c + dc, 2), lax.rem(x + dx, 4), lax.rem(y + dy, 4)
         plane.append((pc * 16 + px * 4 + py, (z * 8 + py * 2 + pc, px)))
     z_peers = [(lax.rem(z + d, 8) * 8 + y * 2 + c, x) for d in range(1, 8)]
+    own_rows = pl.ds(pl.multiple_of(x * RANK, RANK), RANK)
+
+    def columns(member):
+        return pl.ds(pl.multiple_of(member * SHARE, 128), SHARE)
+
+    fetched = [
+        pltpu.make_async_copy(weighted, weighted_in, local_sem.at[0]),
+        pltpu.make_async_copy(rows.at[:, columns(x)], rows_in.at[own_rows, :], local_sem.at[1]),
+    ]
+    for one in fetched:
+        one.start()
     barrier = pltpu.get_barrier_semaphore()
     for peer in [where for _, where in plane] + z_peers:
         pl.semaphore_signal(barrier, inc=1, device_id=peer, device_id_type=MESH)
@@ -442,35 +459,16 @@
             for i, (owner, where) in enumerate(plane)
         ]
     )
-    own_rows = pl.ds(pl.multiple_of(x * RANK, RANK), RANK)
-
-    def columns(member):
-        return pl.ds(pl.multiple_of(member * SHARE, 128), SHARE)
-
-    moved = [
-        copy(
-            rows.at[:, columns(lax.rem(x + hop, 4))],
-            rows_out.at[own_rows, :],
-            rows_send,
-            rows_recv,
-            hop - 1,
-            (s, lax.rem(x + hop, 4)),
-        )
-        for hop in (2, 1, 3)
-    ]
     piece = inp[me]
     for i in range(31):
         piece = piece + r_plane[i]
     r_z[z] = piece
-    around = [
-        copy(r_z.at[z], r_z.at[z], z_send, z_recv, d - 1, z_peers[d - 1])
-        for d in (4, 3, 5, 2, 6, 1, 7)
-    ]
-    for one in around + moved:
-        one.start()
-    rows_out[own_rows, :] = rows[:, columns(x)]
-    for one in around:
-        one.wait()
+    run(
+        [
+            copy(r_z.at[z], r_z.at[z], z_send, z_recv, d - 1, z_peers[d - 1])
+            for d in (4, 3, 5, 2, 6, 1, 7)
+        ]
+    )
     piece = r_z[0]
     for i in range(1, 8):
         piece = piece + r_z[i]
@@ -481,22 +479,54 @@
             for i, (_, where) in enumerate(plane)
         ]
     )
+
+    moved = [
+        copy(
+            rows.at[:, columns(lax.rem(x + hop, 4))],
+            rows_in.at[own_rows, :],
+            rows_send,
+            rows_recv,
+            hop - 1,
+            (s, lax.rem(x + hop, 4)),
+        )
+        for hop in (2, 1, 3)
+    ]
+    for one in moved:
+        one.start()
+
+    above[...] = jnp.zeros_like(above)
+    gram = [jnp.concatenate([out[8 * b + i] for i in range(8)], axis=0) for b in range(4)]
+    second = [found.astype(F32) for found in compress([gram[0], gram[3]])]
+    for p in range(2):
+        above[pl.ds(p * RANK, RANK), pl.ds(p * ROWS, ROWS)] = second[p]
+    mixed = [
+        jnp.concatenate([dot_nn(second[p], gram[2 * p + q]) for q in range(2)], axis=1)
+        for p in range(2)
+    ]
+    last = compress([dot_nt(jnp.concatenate(mixed, axis=0), above[...])])[0]
+    mix = dot_nn(last.astype(F32), above[...]).astype(BF16)
+    for one in fetched:
+        one.wait()
+    weighted_out[...] = jnp.dot(mix, weighted_in[...], preferred_element_type=F32).astype(BF16)
     for one in moved:
         one.wait()
-
-
-def all_reduce(gram, rows):
+    rows_out[...] = jnp.dot(mix, rows_in[...], preferred_element_type=F32).astype(BF16)
+
+
+def merge(gram, rows, weighted):
     shape = (32, PIECE, 128)
     vmem = pl.BlockSpec(memory_space=pltpu.VMEM)
-    total, gathered = pl.pallas_call(
-        reduce_kernel,
-        out_shape=(
-            jax.ShapeDtypeStruct(shape, F32),
-            jax.ShapeDtypeStruct((N_TM * RANK, SHARE), BF16),
-        ),
-        in_specs=[vmem, vmem],
+    anywhere = pl.BlockSpec(memory_space=pl.ANY)
+    return pl.pallas_call(
+        merge_kernel,
+        out_shape=(jax.ShapeDtypeStruct((RANK, SHARE), BF16),) * 2,
+        in_specs=[vmem, anywhere, anywhere],
         out_specs=(vmem, vmem),
         scratch_shapes=[
+            pltpu.VMEM(shape, F32),
+            pltpu.VMEM((N_TM * RANK, SHARE), BF16),
+            pltpu.VMEM((N_TM * RANK, SHARE), BF16),
+            pltpu.VMEM((2 * RANK, 2 * ROWS), F32),
             pltpu.VMEM((31, PIECE, 128), F32),
             pltpu.VMEM((8, PIECE, 128), F32),
             pltpu.SemaphoreType.DMA((62,)),
@@ -505,44 +535,17 @@
             pltpu.SemaphoreType.DMA((7,)),
             pltpu.SemaphoreType.DMA((3,)),
             pltpu.SemaphoreType.DMA((3,)),
+            pltpu.SemaphoreType.DMA((2,)),
         ],
         compiler_params=pltpu.CompilerParams(collective_id=1, has_side_effects=True),
-        name="all_reduce",
-    )(gram.reshape(shape), rows)
-    return total.reshape(4, ROWS, ROWS), gathered
-
-
-def merge_kernel(gram, rows, weighted, rows_out, weighted_out, above):
-    above[...] = jnp.zeros_like(above)
-    second = [c.astype(F32) for c in compress([gram[0], gram[3]])]
-    for p in range(2):
-        above[pl.ds(p * RANK, RANK), pl.ds(p * ROWS, ROWS)] = second[p]
-    mixed = [
-        jnp.concatenate([dot_nn(second[p], gram[2 * p + q]) for q in range(2)], axis=1)
-        for p in range(2)
-    ]
-    last = compress([dot_nt(jnp.concatenate(mixed, axis=0), above[...])])[0]
-    mix = dot_nn(last.astype(F32), above[...]).astype(BF16)
-    rows_out[...] = jnp.dot(mix, rows[...], preferred_element_type=F32).astype(BF16)
-    weighted_out[...] = jnp.dot(mix, weighted[...], preferred_element_type=F32).astype(BF16)
-
-
-def merge(gram, rows, weighted):
-    vmem = pl.BlockSpec(memory_space=pltpu.VMEM)
-    return pl.pallas_call(
-        merge_kernel,
-        out_shape=(jax.ShapeDtypeStruct((RANK, SHARE), BF16),) * 2,
-        in_specs=[vmem] * 3,
-        out_specs=(vmem, vmem),
-        scratch_shapes=[pltpu.VMEM((2 * RANK, 2 * ROWS), F32)],
         name="merge",
-    )(gram, rows, weighted)
+    )(gram.reshape(shape), rows, weighted)
 
 
 def shards(snapshots, prior_basis, mass_factor, neighbours):
     tile = tiles_of(neighbours, lax.axis_index("space"))
     rows, weighted, gram = lowest(tile, prior_basis, snapshots, mass_factor)
-    return merge(*all_reduce(gram, rows), weighted)
+    return merge(gram, rows, weighted)
 
 
 def solution(mesh):

time: 101 us -> 95.1 us (0.942)
  Pallas kernels: 98.8 us -> 89.1 us
  local copies, waits for them, and re-layouts: 0.23 us -> 3.57 us
    pallas_call x1 -> x0, Pallas kernels: 30.1 us -> none  [all_reduce(): pl.pallas_call(reduce_kernel, out_shape=(jax.ShapeDtypeStruct(shape, F32)...]
    pallas_call x1, Pallas kernels: 19 us -> 39.4 us  [merge(): pl.pallas_call(merge_kernel, out_shape=(jax.ShapeDtypeStruct((RANK, SHARE...]
    unnamed x0 -> x2, local copies, waits for them, and re-layouts: none -> 3.34 us
where the time goes in v1:
time: 95.1 us; the launch traced here: 94.8 us
  Pallas kernels  89.1 us (94%)
  local copies, waits for them, and re-layouts  3.57 us (4%)
  other arithmetic  1.42 us (1%)
    pallas_call x1, Pallas kernels, lowest(): pl.pallas_call(lowest_kernel, out_shape=(jax.ShapeDtypeStruct((RANK, SLAB...  49.7 us
    pallas_call x1, Pallas kernels, merge(): pl.pallas_call(merge_kernel, out_shape=(jax.ShapeDtypeStruct((RANK, SHARE...  39.4 us
    unnamed x2, local copies, waits for them, and re-layouts  3.34 us

profile of v1, /device:TPU:1, one launch (start us, length us, event | category | flops | bytes accessed | tf_op | source)
XLA Modules:
  0.0 94.8 jit_solution(12958148668194048441)
XLA Ops:
  0.6 0.7 subtract_shift-right-arithmetic_fusion
  1.3 0.1 copy.15
  1.5 0.1 copy.13
  1.6 0.7 multiply_add_fusion.tile
  2.3 49.7 %lowest.1 = (bf16[64,8192]{1,0:T(8,128)(2,1)}, bf16[256,2048]{1,0:T(8,128)(2,1)}, f32[4,128,128]{2,1,0:T(8,128)}) custom-call(s32[128,7]{1,0:T(8,128)} %multiply_add_fusion.tile, bf16[64,8192]{1,0:T(8,128)(2,1)} %prior.1, bf16[64,8192]{1,0:T(8,128)(2,1)} %snaps.1, bf16[7,64,8192]{2,1,0:T(8,128)(2,1)} %mass.1), custom_call_target="tpu_custom_call" | custom-call | tf_op jit(solution)/shard_map/lowest/pallas_call | solution.py:358
  52.0 39.4 %merge.1 = (bf16[64,2048]{1,0:T(8,128)(2,1)}, bf16[64,2048]{1,0:T(8,128)(2,1)}) custom-call(f32[32,16,128]{2,1,0:T(8,128)} %bitcast.1, bf16[64,8192]{1,0:T(8,128)(2,1)} %get-tuple-element.6.rows, bf16[256,2048]{1,0:T(8,128)(2,1)} %get-tuple-element.7.weighted), custom_call_target="tpu_custom_call" | custom-call | tf_op jit(solution)/shard_map/merge/pallas_call | solution.py:520
  91.4 1.7 %copy.18 = bf16[64,2048]{1,0:T(8,128)(2,1)} copy(bf16[64,2048]{1,0:T(8,128)(2,1)} %get-tuple-element.12) | data formatting | bytes 524288
  93.1 1.7 %copy.19 = bf16[64,2048]{1,0:T(8,128)(2,1)} copy(bf16[64,2048]{1,0:T(8,128)(2,1)} %get-tuple-element.13) | data formatting | bytes 524288
  (1 shorter events, 0.0 us)

commit v2 on v0

--- a/solution.py
+++ b/solution.py
@@ -154,14 +154,13 @@
     tiles[WIDE_TILES + last + 1] = halves(end, end)
 
 
-def lowest_kernel(
+def whole_kernel(
     tile,
     prior,
     snaps,
     mass,
     rows_out,
     weighted_out,
-    gram_out,
     own,
     own_tiles,
     weights_own,
@@ -172,11 +171,25 @@
     r_z,
     total,
     coefs,
+    basis_rows,
+    rows_in,
+    weighted,
+    gram_all,
+    r_wide,
+    r_z_all,
+    total_all,
+    above,
     send_sem,
     recv_sem,
     local_sem,
     sum_send,
     sum_recv,
+    wide_send,
+    wide_recv,
+    all_z_send,
+    all_z_recv,
+    rows_send,
+    rows_recv,
 ):
     s = lax.axis_index("space")
     t = lax.axis_index("tm")
@@ -219,11 +232,18 @@
         plane.append((pc * 4 + py, (space_of(z, py, pc), t)))
     z_peers = [(space_of(lax.rem(z + d, 8), y, c), t) for d in range(1, 8)]
 
+    place = c * 16 + t * 4 + y
+    hops = [(dc, dx, dy) for dx in (2, 1, 3, 0) for dy in (2, 1, 3, 0) for dc in (1, 0)]
+    wide = []
+    for dc, dx, dy in hops[:-1]:
+        pc, px, py = lax.rem(c + dc, 2), lax.rem(t + dx, 4), lax.rem(y + dy, 4)
+        wide.append((pc * 16 + px * 4 + py, (z * 8 + py * 2 + pc, px)))
     barrier = pltpu.get_barrier_semaphore()
-    for peer in x_peers + [where for _, where in plane] + z_peers + [(up, t), (down, t)]:
+    planes = [where for _, where in plane + wide]
+    for peer in x_peers + planes + z_peers + [(up, t), (down, t)]:
         pl.semaphore_signal(barrier, inc=1, device_id=peer, device_id_type=MESH)
 
-    pl.semaphore_wait(barrier, 19)
+    pl.semaphore_wait(barrier, 50)
 
     def remote(src, dst, slot, peer, part):
         return pltpu.make_async_remote_copy(
@@ -325,15 +345,15 @@
     for one in passed:
         one.start()
 
-    rows_out[...] = jnp.dot(
+    basis_rows[...] = jnp.dot(
         coefs[t], own[:, pl.ds(HALO, SLAB)], preferred_element_type=F32
     ).astype(BF16)
     for hop in (1, 3, 2):
         share(hop).wait()
 
-    def put(group, weighted):
-        weighted_out[pl.ds(pl.multiple_of(group * RANK, RANK), RANK), :] = jnp.dot(
-            coefs[group], weighted, preferred_element_type=F32
+    def put(group, block):
+        weighted[pl.ds(pl.multiple_of(group * RANK, RANK), RANK), :] = jnp.dot(
+            coefs[group], block, preferred_element_type=F32
         ).astype(BF16)
 
     put(t, weights_own[:, pl.ds(pl.multiple_of(t * SHARE, 128), SHARE)])
@@ -343,27 +363,99 @@
         put(lax.rem(t + N_TM - hop, N_TM), weights_in[hop - 1])
     for a in range(2):
         for b in range(2):
-            gram_out[2 * a + b] = lax.dot_general(
-                weighted_out[pl.ds(a * ROWS, ROWS), :],
-                weighted_out[pl.ds(b * ROWS, ROWS), :],
+            local = lax.dot_general(
+                weighted[pl.ds(a * ROWS, ROWS), :],
+                weighted[pl.ds(b * ROWS, ROWS), :],
                 (((1,), (1,)), ((), ())),
                 preferred_element_type=F32,
             )
-
-
-def lowest(tile, prior, snaps, mass):
+            for i in range(8):
+                gram_all[8 * (2 * a + b) + i] = local[16 * i : 16 * i + 16, :]
+
+    def copy(src, dst, send, recv, slot, peer):
+        return pltpu.make_async_remote_copy(
+            src_ref=src,
+            dst_ref=dst,
+            send_sem=send.at[slot],
+            recv_sem=recv.at[slot],
+            device_id=peer,
+            device_id_type=MESH,
+        )
+
+    run(
+        [
+            copy(gram_all.at[owner], r_wide.at[i], wide_send, wide_recv, i, where)
+            for i, (owner, where) in enumerate(wide)
+        ]
+    )
+    piece = gram_all[place]
+    for i in range(31):
+        piece = piece + r_wide[i]
+    r_z_all[z] = piece
+    run(
+        [
+            copy(r_z_all.at[z], r_z_all.at[z], all_z_send, all_z_recv, d - 1, z_peers[d - 1])
+            for d in (4, 3, 5, 2, 6, 1, 7)
+        ]
+    )
+    piece = r_z_all[0]
+    for i in range(1, 8):
+        piece = piece + r_z_all[i]
+    total_all[place] = piece
+    run(
+        [
+            copy(total_all.at[place], total_all.at[place], wide_send, wide_recv, 31 + i, where)
+            for i, (_, where) in enumerate(wide)
+        ]
+    )
+
+    own_rows = pl.ds(pl.multiple_of(t * RANK, RANK), RANK)
+
+    def columns(member):
+        return pl.ds(pl.multiple_of(member * SHARE, 128), SHARE)
+
+    moved = [
+        copy(
+            basis_rows.at[:, columns(lax.rem(t + hop, 4))],
+            rows_in.at[own_rows, :],
+            rows_send,
+            rows_recv,
+            hop - 1,
+            (s, lax.rem(t + hop, 4)),
+        )
+        for hop in (2, 1, 3)
+    ]
+    for one in moved:
+        one.start()
+
+    rows_in[own_rows, :] = basis_rows[:, columns(t)]
+    above[...] = jnp.zeros_like(above)
+    grams = [jnp.concatenate([total_all[8 * b + i] for i in range(8)], axis=0) for b in range(4)]
+    second = [found.astype(F32) for found in compress([grams[0], grams[3]])]
+    for p in range(2):
+        above[pl.ds(p * RANK, RANK), pl.ds(p * ROWS, ROWS)] = second[p]
+    mixed = [
+        jnp.concatenate([dot_nn(second[p], grams[2 * p + q]) for q in range(2)], axis=1)
+        for p in range(2)
+    ]
+    last = compress([dot_nt(jnp.concatenate(mixed, axis=0), above[...])])[0]
+    mix = dot_nn(last.astype(F32), above[...]).astype(BF16)
+    weighted_out[...] = jnp.dot(mix, weighted[...], preferred_element_type=F32).astype(BF16)
+    for one in moved:
+        one.wait()
+    rows_out[...] = jnp.dot(mix, rows_in[...], preferred_element_type=F32).astype(BF16)
+
+
+def merged(tile, prior, snaps, mass):
     piece = (16, 128)
     vmem = pl.BlockSpec(memory_space=pltpu.VMEM)
     anywhere = pl.BlockSpec(memory_space=pl.ANY)
+    semaphores = [(8, 2), (8, 2), (6,), (21,), (21,), (62,), (62,), (7,), (7,), (3,), (3,)]
     return pl.pallas_call(
-        lowest_kernel,
-        out_shape=(
-            jax.ShapeDtypeStruct((RANK, SLAB), BF16),
-            jax.ShapeDtypeStruct((N_TM * RANK, SHARE), BF16),
-            jax.ShapeDtypeStruct((4, ROWS, ROWS), F32),
-        ),
+        whole_kernel,
+        out_shape=(jax.ShapeDtypeStruct((RANK, SHARE), BF16),) * 2,
         in_specs=[pl.BlockSpec(memory_space=pltpu.SMEM), anywhere, anywhere, anywhere],
-        out_specs=(vmem, vmem, vmem),
+        out_specs=(vmem, vmem),
         scratch_shapes=[
             pltpu.VMEM((ROWS, WIDE), BF16),
             pltpu.VMEM((2 * WIDE_TILES + 1, ROWS, 128), BF16),
@@ -375,174 +467,40 @@
             pltpu.VMEM((8,) + piece, F32),
             pltpu.VMEM((8,) + piece, F32),
             pltpu.VMEM((N_TM, RANK, ROWS), BF16),
-            pltpu.SemaphoreType.DMA((8, 2)),
-            pltpu.SemaphoreType.DMA((8, 2)),
-            pltpu.SemaphoreType.DMA((6,)),
-            pltpu.SemaphoreType.DMA((21,)),
-            pltpu.SemaphoreType.DMA((21,)),
-        ],
+            pltpu.VMEM((RANK, SLAB), BF16),
+            pltpu.VMEM((N_TM * RANK, SHARE), BF16),
+            pltpu.VMEM((N_TM * RANK, SHARE), BF16),
+            pltpu.VMEM((32,) + piece, F32),
+            pltpu.VMEM((31,) + piece, F32),
+            pltpu.VMEM((8,) + piece, F32),
+            pltpu.VMEM((32,) + piece, F32),
+            pltpu.VMEM((2 * RANK, 2 * ROWS), F32),
+        ]
+        + [pltpu.SemaphoreType.DMA(shape) for shape in semaphores],
         compiler_params=pltpu.CompilerParams(collective_id=0, has_side_effects=True),
-        name="lowest",
+        name="merged",
     )(tile, prior, snaps, mass)
 
 
-PIECE = 16
-
-
-def reduce_kernel(
-    inp,
-    rows,
-    out,
-    rows_out,
-    r_plane,
-    r_z,
-    plane_send,
-    plane_recv,
-    z_send,
-    z_recv,
-    rows_send,
-    rows_recv,
-):
-    s = lax.axis_index("space")
-    x = lax.axis_index("tm")
-    c = lax.rem(s, 2)
-    y = lax.rem(s // 2, 4)
-    z = s // 8
-    me = c * 16 + x * 4 + y
-    hops = [(dc, dx, dy) for dx in (2, 1, 3, 0) for dy in (2, 1, 3, 0) for dc in (1, 0)]
-    plane = []
-    for dc, dx, dy in hops[:-1]:
-        pc, px, py = lax.rem(c + dc, 2), lax.rem(x + dx, 4), lax.rem(y + dy, 4)
-        plane.append((pc * 16 + px * 4 + py, (z * 8 + py * 2 + pc, px)))
-    z_peers = [(lax.rem(z + d, 8) * 8 + y * 2 + c, x) for d in range(1, 8)]
-    barrier = pltpu.get_barrier_semaphore()
-    for peer in [where for _, where in plane] + z_peers:
-        pl.semaphore_signal(barrier, inc=1, device_id=peer, device_id_type=MESH)
-    pl.semaphore_wait(barrier, 38)
-
-    def copy(src, dst, send, recv, slot, peer):
-        return pltpu.make_async_remote_copy(
-            src_ref=src,
-            dst_ref=dst,
-            send_sem=send.at[slot],
-            recv_sem=recv.at[slot],
-            device_id=peer,
-            device_id_type=MESH,
-        )
-
-    def run(copies):
-        for one in copies:
-            one.start()
-        for one in copies:
-            one.wait()
-
-    run(
-        [
-            copy(inp.at[owner], r_plane.at[i], plane_send, plane_recv, i, where)
-            for i, (owner, where) in enumerate(plane)
-        ]
-    )
-    own_rows = pl.ds(pl.multiple_of(x * RANK, RANK), RANK)
-
-    def columns(member):
-        return pl.ds(pl.multiple_of(member * SHARE, 128), SHARE)
-
-    moved = [
-        copy(
-            rows.at[:, columns(lax.rem(x + hop, 4))],
-            rows_out.at[own_rows, :],
-            rows_send,
-            rows_recv,
-            hop - 1,
-            (s, lax.rem(x + hop, 4)),
-        )
-        for hop in (2, 1, 3)
-    ]
-    piece = inp[me]
-    for i in range(31):
-        piece = piece + r_plane[i]
-    r_z[z] = piece
-    around = [
-        copy(r_z.at[z], r_z.at[z], z_send, z_recv, d - 1, z_peers[d - 1])
-        for d in (4, 3, 5, 2, 6, 1, 7)
-    ]
-    for one in around + moved:
-        one.start()
-    rows_out[own_rows, :] = rows[:, columns(x)]
-    for one in around:
-        one.wait()
-    piece = r_z[0]
-    for i in range(1, 8):
-        piece = piece + r_z[i]
-    out[me] = piece
-    run(
-        [
-            copy(out.at[me], out.at[me], plane_send, plane_recv, 31 + i, where)
-            for i, (_, where) in enumerate(plane)
-        ]
-    )
-    for one in moved:
-        one.wait()
-
-
-def all_reduce(gram, rows):
-    shape = (32, PIECE, 128)
+def pass_kernel(rows, weighted, rows_out, weighted_out):
+    rows_out[...] = rows[...]
+    weighted_out[...] = weighted[...]
+
+
+def handed(rows, weighted):
     vmem = pl.BlockSpec(memory_space=pltpu.VMEM)
-    total, gathered = pl.pallas_call(
-        reduce_kernel,
-        out_shape=(
-            jax.ShapeDtypeStruct(shape, F32),
-            jax.ShapeDtypeStruct((N_TM * RANK, SHARE), BF16),
-        ),
+    return pl.pallas_call(
+        pass_kernel,
+        out_shape=(jax.ShapeDtypeStruct((RANK, SHARE), BF16),) * 2,
         in_specs=[vmem, vmem],
         out_specs=(vmem, vmem),
-        scratch_shapes=[
-            pltpu.VMEM((31, PIECE, 128), F32),
-            pltpu.VMEM((8, PIECE, 128), F32),
-            pltpu.SemaphoreType.DMA((62,)),
-            pltpu.SemaphoreType.DMA((62,)),
-            pltpu.SemaphoreType.DMA((7,)),
-            pltpu.SemaphoreType.DMA((7,)),
-            pltpu.SemaphoreType.DMA((3,)),
-            pltpu.SemaphoreType.DMA((3,)),
-        ],
-        compiler_params=pltpu.CompilerParams(collective_id=1, has_side_effects=True),
-        name="all_reduce",
-    )(gram.reshape(shape), rows)
-    return total.reshape(4, ROWS, ROWS), gathered
-
-
-def merge_kernel(gram, rows, weighted, rows_out, weighted_out, above):
-    above[...] = jnp.zeros_like(above)
-    second = [c.astype(F32) for c in compress([gram[0], gram[3]])]
-    for p in range(2):
-        above[pl.ds(p * RANK, RANK), pl.ds(p * ROWS, ROWS)] = second[p]
-    mixed = [
-        jnp.concatenate([dot_nn(second[p], gram[2 * p + q]) for q in range(2)], axis=1)
-        for p in range(2)
-    ]
-    last = compress([dot_nt(jnp.concatenate(mixed, axis=0), above[...])])[0]
-    mix = dot_nn(last.astype(F32), above[...]).astype(BF16)
-    rows_out[...] = jnp.dot(mix, rows[...], preferred_element_type=F32).astype(BF16)
-    weighted_out[...] = jnp.dot(mix, weighted[...], preferred_element_type=F32).astype(BF16)
-
-
-def merge(gram, rows, weighted):
-    vmem = pl.BlockSpec(memory_space=pltpu.VMEM)
-    return pl.pallas_call(
-        merge_kernel,
-        out_shape=(jax.ShapeDtypeStruct((RANK, SHARE), BF16),) * 2,
-        in_specs=[vmem] * 3,
-        out_specs=(vmem, vmem),
-        scratch_shapes=[pltpu.VMEM((2 * RANK, 2 * ROWS), F32)],
-        name="merge",
-    )(gram, rows, weighted)
+        name="handed",
+    )(rows, weighted)
 
 
 def shards(snapshots, prior_basis, mass_factor, neighbours):
     tile = tiles_of(neighbours, lax.axis_index("space"))
-    rows, weighted, gram = lowest(tile, prior_basis, snapshots, mass_factor)
-    return merge(*all_reduce(gram, rows), weighted)
+    return handed(*merged(tile, prior_basis, snapshots, mass_factor))
 
 
 def solution(mesh):

time: 101 us -> 88.3 us (0.87)
  Pallas kernels: 98.8 us -> 85.8 us
    pallas_call x3 -> x2, Pallas kernels: 98.8 us -> 85.8 us  [the longest x1 83.9 us: merged(): pl.pallas_call(whole_kernel, out_shape=(jax.ShapeDtypeStruct((RANK, SHARE...]
where the time goes in v2:
time: 88.3 us; the launch traced here: 88.1 us
  Pallas kernels  85.8 us (97%)
  other arithmetic  1.42 us (2%)
    pallas_call x1, Pallas kernels, merged(): pl.pallas_call(whole_kernel, out_shape=(jax.ShapeDtypeStruct((RANK, SHARE...  83.9 us
    pallas_call x1, Pallas kernels, handed(): pl.pallas_call(pass_kernel, out_shape=(jax.ShapeDtypeStruct((RANK, SHARE)...  1.84 us

profile of v2, /device:TPU:1, one launch (start us, length us, event | category | flops | bytes accessed | tf_op | source)
XLA Modules:
  0.0 88.1 jit_solution(5258249537072159941)
XLA Ops:
  0.6 0.7 subtract_shift-right-arithmetic_fusion
  1.3 0.1 copy.15
  1.5 0.1 copy.13
  1.6 0.7 multiply_add_fusion.tile
  2.3 83.9 %merged.1 = (bf16[64,2048]{1,0:T(8,128)(2,1)}, bf16[64,2048]{1,0:T(8,128)(2,1)}) custom-call(s32[128,7]{1,0:T(8,128)} %multiply_add_fusion.tile, bf16[64,8192]{1,0:T(8,128)(2,1)} %prior.1, bf16[64,8192]{1,0:T(8,128)(2,1)} %snaps.1, bf16[7,64,8192]{2,1,0:T(8,128)(2,1)} %mass.1), custom_call_target="tpu_custom_call" | custom-call | tf_op jit(solution)/shard_map/merged/pallas_call | solution.py:454
  86.2 1.8 %handed.1 = (bf16[64,2048]{1,0:T(8,128)(2,1)}, bf16[64,2048]{1,0:T(8,128)(2,1)}) custom-call(bf16[64,2048]{1,0:T(8,128)(2,1)} %get-tuple-element.4.rows, bf16[64,2048]{1,0:T(8,128)(2,1)} %get-tuple-element.5.weighted), custom_call_target="tpu_custom_call" | custom-call | tf_op jit(solution)/shard_map/handed/pallas_call | solution.py:492
  (1 shorter events, 0.0 us)

commit v3 on v2

--- a/solution.py
+++ b/solution.py
@@ -106,8 +106,8 @@
 
 
 def tiles_of(neighbours, s):
-    at = neighbours - (s * LOCAL_BLOCKS - REACH)
-    second = lax.broadcasted_iota(jnp.int32, at.shape, 0) & 1
+    at = neighbours.T - (s * LOCAL_BLOCKS - REACH)
+    second = lax.broadcasted_iota(jnp.int32, at.shape, 1) & 1
     moved = (at & 1) ^ second
     return ((at + 1 - second) >> 1) + moved * WIDE_TILES
 
@@ -115,8 +115,8 @@
 def pick_modes(tile, j, tiles, in_low):
     picks = []
     for k in range(NEIGHBOURS):
-        low = tiles[tile[2 * j, k]]
-        high = tiles[tile[2 * j + 1, k]]
+        low = tiles[tile[k, 2 * j]]
+        high = tiles[tile[k, 2 * j + 1]]
         picks.append(jnp.where(in_low, low, high))
     return jnp.concatenate(picks, axis=1)
 
@@ -216,7 +216,7 @@
             factor.at[:, :, pl.ds(chunk * i, chunk)],
             local_sem.at[2 + i],
         )
-        for i in range(4)
+        for i in (1, 2, 0, 3)
     ]
     for one in loads + fetches:
         one.start()
@@ -256,11 +256,12 @@
         )
 
     def share(hop):
+        target = lax.rem(t + hop, 4)
         return remote(
-            weights_own.at[:, pl.ds(pl.multiple_of(lax.rem(t + hop, 4) * SHARE, 128), SHARE)],
+            weights_own.at[:, pl.ds(pl.multiple_of(target * SHARE, 128), SHARE)],
             weights_in.at[hop - 1],
             hop - 1,
-            x_peers[hop - 1],
+            (s, target),
             0,
         )
 
@@ -282,15 +283,6 @@
     for one in loads:
         one.wait()
     widen(own, own_tiles, HALO_TILES + 1, WIDE_TILES - HALO_TILES, 9)
-    for part in range(2):
-        for side in range(2):
-            own_edge(part, side).wait()
-    widen(own, own_tiles, 1, HALO_TILES + 1, HALO_TILES)
-    widen(own, own_tiles, WIDE_TILES - HALO_TILES, WIDE_TILES, HALO_TILES)
-    widen_ends(own, own_tiles)
-    for one in fetches:
-        one.wait()
-
     def own_quarter(quarter):
         def own_tile(i, carry):
             j = quarter * (SHARE_BLOCKS // 2) + i
@@ -301,10 +293,25 @@
 
         lax.fori_loop(0, SHARE_BLOCKS // 2, own_tile, 0, unroll=4)
 
-    for hop in (2, 1, 3):
-        own_quarter(lax.rem(t + hop, 4))
-        share(hop).start()
-    own_quarter(t)
+    def send_quarter(quarter):
+        for g in range(N_TM):
+            if g != quarter:
+
+                @pl.when(t == g)
+                def _():
+                    share((quarter - g) % N_TM).start()
+
+    for at, quarter in enumerate((1, 2, 0, 3)):
+        if at == 2:
+            for part in range(2):
+                for side in range(2):
+                    own_edge(part, side).wait()
+            widen(own, own_tiles, 1, HALO_TILES + 1, HALO_TILES)
+            widen(own, own_tiles, WIDE_TILES - HALO_TILES, WIDE_TILES, HALO_TILES)
+            widen_ends(own, own_tiles)
+        fetches[at].wait()
+        own_quarter(quarter)
+        send_quarter(quarter)
     local = lax.dot_general(
         weights_own[...], weights_own[...], (((1,), (1,)), ((), ())), preferred_element_type=F32
     )

time: 88.3 us -> 86.1 us (0.975)
  Pallas kernels: 85.8 us -> 84 us
    pallas_call x1, Pallas kernels: 83.9 us -> 82.2 us  [merged(): pl.pallas_call(whole_kernel, out_shape=(jax.ShapeDtypeStruct((RANK, SHARE...]
where the time goes in v3:
time: 86.1 us; the launch traced here: 86 us
  Pallas kernels  84 us (98%)
  other arithmetic  1.29 us (1%)
    pallas_call x1, Pallas kernels, merged(): pl.pallas_call(whole_kernel, out_shape=(jax.ShapeDtypeStruct((RANK, SHARE...  82.2 us
    pallas_call x1, Pallas kernels, handed(): pl.pallas_call(pass_kernel, out_shape=(jax.ShapeDtypeStruct((RANK, SHARE)...  1.84 us

profile of v3, /device:TPU:1, one launch (start us, length us, event | category | flops | bytes accessed | tf_op | source)
XLA Modules:
  0.0 86.0 jit_solution(16572131860673498647)
XLA Ops:
  0.6 1.3 %add_bitcast_fusion.tile = s32[7,128]{1,0:T(8,128)} fusion(s32[128,7]{0,1:T(8,128)} %param.7, s32[128]{0:T(128)S(1)} %iota_and_fusion, s32[]{:T(128)S(6)} %sub.14), kind=kLoop, calls=%fused_computation | loop fusion | flops 7168 | bytes 7684 | tf_op jit(solution)/shard_map/add | solution.py:112
  1.9 82.2 %merged.1 = (bf16[64,2048]{1,0:T(8,128)(2,1)}, bf16[64,2048]{1,0:T(8,128)(2,1)}) custom-call(s32[7,128]{1,0:T(8,128)} %add_bitcast_fusion.tile, bf16[64,8192]{1,0:T(8,128)(2,1)} %prior.1, bf16[64,8192]{1,0:T(8,128)(2,1)} %snaps.1, bf16[7,64,8192]{2,1,0:T(8,128)(2,1)} %mass.1), custom_call_target="tpu_custom_call" | custom-call | tf_op jit(solution)/shard_map/merged/pallas_call | solution.py:461
  84.1 1.8 %handed.1 = (bf16[64,2048]{1,0:T(8,128)(2,1)}, bf16[64,2048]{1,0:T(8,128)(2,1)}) custom-call(bf16[64,2048]{1,0:T(8,128)(2,1)} %get-tuple-element.4.rows, bf16[64,2048]{1,0:T(8,128)(2,1)} %get-tuple-element.5.weighted), custom_call_target="tpu_custom_call" | custom-call | tf_op jit(solution)/shard_map/handed/pallas_call | solution.py:499
  (1 shorter events, 0.0 us)
